TPU v7x, 512 devices: a whole 4x4x16 slice. The times are simulated.
512 devices in a mesh: ep: 16 (over z), mx: 4 (over x), my: 8 (over y, core).
Axes of the slice: x: 4, y: 4, z: 16, core: 2. Of those that a mesh axis runs over, the one named last changes fastest.
Arguments:
- context: bfloat16 [16384, 2048], P(('ep', 'mx')), may hold values from -6 to 6
- resid_in: bfloat16 [16384, 2048], P(('ep', 'mx'), 'my'), may hold values from -70 to 70
- out_weight: bfloat16 [2048, 2048], P(None, 'my'), may hold values from -0.125 to 0.125
- norm_gain: float32 [2048], P('my'), may hold values from 0.5 to 1.5
- gate_weight: bfloat16 [8, 5632, 2048], P(None, ('ep', 'my'), 'mx'), may hold values from -0.125 to 0.125
- up_weight: bfloat16 [8, 5632, 2048], P(None, ('ep', 'my'), 'mx'), may hold values from -0.125 to 0.125
- down_weight: bfloat16 [8, 5632, 2048], P(None, ('ep', 'my'), 'mx'), may hold values from -0.078125 to 0.078125
- routes: int32 [16384, 2], P(('ep', 'mx')), may hold values from 0 to 7, all different within a row; in each aligned block of 256 rows (0 to 255, 256 to 511, ...) at most 96 rows name the same one
- gate_probs: float32 [16384, 2], P(('ep', 'mx')), may hold values from 0.05 to 1
- final_gain: float32 [2048], P('my'), may hold values from 0.5 to 1.5
Outputs:
- normed_out: bfloat16 [16384, 2048], P(('ep', 'mx'), 'my')
- stream_out: bfloat16 [16384, 2048], P(('ep', 'mx'), 'my')
Inputs may be any that keep to these rules, and one draw needn't show every extreme that they name: `routes`: each row names 2 different experts; in each aligned block of 256 rows no expert is named by more than 96 rows, a bound that some block reaches.
All inputs are finite; a program needn't handle non-finite values.
Results may differ from a plain program's by a relative error of at most 0.012.
Values may be sent and summed in bfloat16 or wider, within the bound.
A program may use at most 128 MiB of HBM per device.

v0:
```python
import jax
import jax.numpy as jnp
import numpy as np
from jax import lax
from jax.sharding import PartitionSpec as P

D = 2048
EXPERTS = 8
TOPK = 2
MOST = 96
EPSILON = 1e-06


def row_scale(stream_f):
    partial_sq = jnp.sum(stream_f * stream_f, axis=1)
    row_total = lax.psum(partial_sq, "my")
    return lax.rsqrt(row_total / D + EPSILON)


def shards(
    context,
    resid_in,
    out_weight,
    norm_gain,
    gate_weight,
    up_weight,
    down_weight,
    routes,
    gate_probs,
    final_gain,
):
    ep_count = lax.axis_size("ep")
    slot_dev = max(1, EXPERTS // ep_count)
    slot_total = slot_dev * ep_count
    replicas = slot_total // EXPERTS
    capacity = MOST // replicas
    tok_rows = context.shape[0]
    feat_block = resid_in.shape[1]
    piece_units = gate_weight.shape[1]
    slot_rows = ep_count * capacity
    projected = jnp.dot(context, out_weight, preferred_element_type=jnp.float32)
    stream = (projected + resid_in.astype(jnp.float32)).astype(jnp.bfloat16)
    stream_f = stream.astype(jnp.float32)
    normed = (stream_f * row_scale(stream_f)[:, None] * norm_gain[None, :]).astype(jnp.bfloat16)
    chosen = routes.reshape(-1)
    onehot = (chosen[:, None] == jnp.arange(EXPERTS, dtype=jnp.int32)[None, :]).astype(jnp.int32)
    before = jnp.cumsum(onehot, axis=0) - onehot
    ranking = jnp.sum(before * onehot, axis=1)
    slot_index = chosen * replicas + ranking % replicas
    target = slot_index * capacity + ranking // replicas
    row_ids = jnp.arange(tok_rows * TOPK, dtype=jnp.int32) // TOPK
    source = jnp.full((slot_total * capacity,), tok_rows, jnp.int32).at[target].set(row_ids)
    padded = jnp.concatenate([normed, jnp.zeros((1, feat_block), jnp.bfloat16)], axis=0)
    packed = padded[source].reshape(ep_count, slot_dev, capacity, feat_block)
    landed = lax.all_to_all(packed, "ep", split_axis=0, concat_axis=0, tiled=True)
    gathered = lax.all_gather(landed, "my", axis=3, tiled=True)
    expert_table = (
        np.arange(ep_count)[:, None] * slot_dev + np.arange(slot_dev)[None, :]
    ) // replicas

    def fetch(weight, after):
        chosen_rows, _ = lax.optimization_barrier((weight[expert_table], after))
        got = lax.all_to_all(chosen_rows, "ep", split_axis=0, concat_axis=0, tiled=True)
        wide = lax.all_gather(got, "mx", axis=3, tiled=True)
        return (got, jnp.transpose(wide, (1, 0, 2, 3)).reshape(slot_dev, ep_count * piece_units, D))

    raw_gate, w_gate = fetch(gate_weight, landed)
    raw_up, w_up = fetch(up_weight, raw_gate)
    _, w_down = fetch(down_weight, raw_up)
    tokens_in = jnp.transpose(gathered, (1, 0, 2, 3)).reshape(slot_dev, slot_rows, D)
    gate_proj = jnp.einsum("srd,sfd->srf", tokens_in, w_gate, preferred_element_type=jnp.float32)
    up_proj = jnp.einsum("srd,sfd->srf", tokens_in, w_up, preferred_element_type=jnp.float32)
    hidden = (jax.nn.silu(gate_proj) * up_proj).astype(jnp.bfloat16)
    expert_out = jnp.einsum("srf,sfd->srd", hidden, w_down, preferred_element_type=jnp.float32)
    summed = lax.psum_scatter(
        expert_out.astype(jnp.bfloat16), "my", scatter_dimension=2, tiled=True
    )
    sent_back = summed.reshape(slot_dev, ep_count, capacity, feat_block)
    sent_back = jnp.transpose(sent_back, (1, 0, 2, 3))
    returned = lax.all_to_all(sent_back, "ep", split_axis=0, concat_axis=0, tiled=True).reshape(
        slot_total * capacity, feat_block
    )
    picked = returned[target].reshape(tok_rows, TOPK, feat_block).astype(jnp.float32)
    weights_norm = gate_probs / jnp.sum(gate_probs, axis=1, keepdims=True)
    mixed = jnp.sum(weights_norm[:, :, None] * picked, axis=1)
    updated = stream_f + mixed
    normed_out = (updated * row_scale(updated)[:, None] * final_gain[None, :]).astype(jnp.bfloat16)
    return (normed_out, updated.astype(jnp.bfloat16))


def solution(mesh):
    placed = (
        P(("ep", "mx"), None),
        P(("ep", "mx"), "my"),
        P(None, "my"),
        P("my"),
        P(None, ("ep", "my"), "mx"),
        P(None, ("ep", "my"), "mx"),
        P(None, ("ep", "my"), "mx"),
        P(("ep", "mx"), None),
        P(("ep", "mx"), None),
        P("my"),
    )
    return jax.shard_map(
        shards,
        mesh=mesh,
        in_specs=placed,
        out_specs=(P(("ep", "mx"), "my"), P(("ep", "mx"), "my")),
        check_vma=False,
    )
```

profile of v0, /device:TPU:2, one launch (start us, length us, event | category | flops | bytes accessed | tf_op | source)
XLA Modules:
  0.0 421.2 jit_solution(16044243208929844896)
XLA Ops:
  10.9 2.4 scatter_custom_fusion
  13.4 1.7 multiply_reduce_fusion.2
  15.2 15.0 %psum.14 = f32[256]{0:T(256)S(1)} all-reduce(f32[256]{0:T(256)S(1)} %get-tuple-element.10), channel_id=1, replica_groups=mesh['ep'=16,'mx'=4,'my'=8] {'my'}, use_global_device_ids=true, to_apply=%region_2.0 | all-reduce | flops 256 | bytes 2048 | tf_op jit(solution)/shard_map/psum | solution.py:16
  30.3 3.3 gather_fusion
  33.6 15.2 %all-to-all-start = ((bf16[16,1,48,256]{3,2,1,0:T(8,128)(2,1)}), bf16[16,1,48,256]{3,2,1,0:T(8,128)(2,1)S(1)}, u32[]{:S(2)}, u32[]{:S(2)}) async-start(bf16[16,1,48,256]{3,2,1,0:T(8,128)(2,1)} %bitcast.5), calls=%async_computation | async-start | bytes 786432 | tf_op jit(solution)/shard_map/all_to_all | solution.py:55
  48.9 2.6 gather_fusion.1
  51.5 18.3 %all-to-all-done = bf16[16,1,48,256]{3,2,1,0:T(8,128)(2,1)S(1)} async-done(((bf16[16,1,48,256]{3,2,1,0:T(8,128)(2,1)}), bf16[16,1,48,256]{3,2,1,0:T(8,128)(2,1)S(1)}, u32[]{:S(2)}, u32[]{:S(2)}) %all-to-all-start) | async-done | bytes 393248 | tf_op jit(solution)/shard_map/all_to_all | solution.py:55
  70.2 46.5 %all_to_all.25 = bf16[16,1,44,512]{3,2,1,0:T(8,128)(2,1)} all-to-all(bf16[16,1,44,512]{3,2,1,0:T(8,128)(2,1)S(1)} %copy.29), channel_id=1, replica_groups=mesh['ep'=16,'mx'=4,'my'=8] {'ep'}, dimensions={0} | all-to-all | bytes 1441792 | tf_op jit(solution)/shard_map/all_to_all | solution.py:63
  117.5 2.6 gather_fusion.2
  120.6 46.5 %all_to_all.26 = bf16[16,1,44,512]{3,2,1,0:T(8,128)(2,1)} all-to-all(bf16[16,1,44,512]{3,2,1,0:T(8,128)(2,1)S(1)} %copy.30), channel_id=1, replica_groups=mesh['ep'=16,'mx'=4,'my'=8] {'ep'}, dimensions={0} | all-to-all | bytes 1441792 | tf_op jit(solution)/shard_map/all_to_all | solution.py:63
  167.3 2.6 gather_fusion.3
  170.4 46.6 %all_to_all.27 = bf16[16,1,44,512]{3,2,1,0:T(8,128)(2,1)} all-to-all(bf16[16,1,44,512]{3,2,1,0:T(8,128)(2,1)S(1)} %copy.31), channel_id=1, replica_groups=mesh['ep'=16,'mx'=4,'my'=8] {'ep'}, dimensions={0} | all-to-all | bytes 1441792 | tf_op jit(solution)/shard_map/all_to_all | solution.py:63
  217.1 4.4 %reshape.169 = bf16[704,2048]{1,0:T(8,128)(2,1)} reshape(bf16[16,1,44,2048]{3,2,1,0:T(8,128)(2,1)} %all-gather.7.cloned.1.call-done) | data formatting | bytes 5767168 | tf_op jit(solution)/shard_map/reshape.8
  221.4 6.9 %fusion.14 = f32[768,704]{0,1:T(8,128)} fusion(bf16[768,2048]{1,0:T(8,128)(2,1)} %bitcast.38, bf16[704,2048]{1,0:T(8,128)(2,1)} %reshape.169), kind=kOutput, calls=%fused_computation.50 | convolution fusion | flops 2214592512 | bytes 8192000 | tf_op jit(solution)/shard_map/srd,sfd->srf/dot_general | solution.py:71
  228.3 22.2 %all-gather.9.cloned.1.call-done = bf16[16,1,44,2048]{3,2,1,0:T(8,128)(2,1)} async-done(((bf16[16,1,44,512]{3,2,1,0:T(8,128)(2,1)}), bf16[16,1,44,2048]{3,2,1,0:T(8,128)(2,1)}) %all-gather.9.cloned.1.call-update) | async-done | bytes 2883600 | tf_op jit(solution)/shard_map/all_gather | solution.py:64
  250.6 4.3 %reshape.170 = bf16[704,2048]{1,0:T(8,128)(2,1)} reshape(bf16[16,1,44,2048]{3,2,1,0:T(8,128)(2,1)} %all-gather.9.cloned.1.call-done) | data formatting | bytes 5767168 | tf_op jit(solution)/shard_map/reshape.15
  254.9 45.1 %all-gather.11.cloned.1.call-done = bf16[16,1,44,2048]{3,2,1,0:T(8,128)(2,1)} async-done(((bf16[16,1,44,512]{3,2,1,0:T(8,128)(2,1)}), bf16[16,1,44,2048]{3,2,1,0:T(8,128)(2,1)}) %all-gather.11.cloned.1.call-update) | async-done | bytes 2883600 | tf_op jit(solution)/shard_map/all_gather | solution.py:64
  300.1 4.4 %reshape.171 = bf16[704,2048]{1,0:T(8,128)(2,1)} reshape(bf16[16,1,44,2048]{3,2,1,0:T(8,128)(2,1)} %all-gather.11.cloned.1.call-done) | data formatting | bytes 5767168 | tf_op jit(solution)/shard_map/reshape.18
  304.4 12.4 %fusion = bf16[1,768,2048]{2,1,0:T(8,128)(2,1)} fusion(bf16[704,2048]{1,0:T(8,128)(2,1)} %reshape.171, f32[768,704]{0,1:T(8,128)} %fusion.14, bf16[768,2048]{1,0:T(8,128)(2,1)} %bitcast.39, bf16[704,2048]{1,0:T(8,128)(2,1)} %reshape.170), kind=kOutput, calls=%fused_computation.7 | convolution fusion | flops 4434001920 | bytes 14221312 | tf_op jit(solution)/shard_map/srf,sfd->srd/dot_general | solution.py:74
  316.9 44.6 %reduce-scatter.2.cloned.1.call-done = bf16[1,768,256]{2,1,0:T(8,128)(2,1)} async-done(((bf16[1,768,2048]{2,1,0:T(8,128)(2,1)}), bf16[1,768,256]{2,1,0:T(8,128)(2,1)}) %reduce-scatter.2.cloned.1.call-update) | async-done | bytes 393232 | tf_op jit(solution)/shard_map/reduce_scatter | solution.py:75
  361.5 12.3 %all-to-all-start.4 = ((bf16[16,1,48,256]{3,2,1,0:T(8,128)(2,1)}), bf16[16,1,48,256]{3,2,1,0:T(8,128)(2,1)S(1)}, u32[]{:S(2)}, u32[]{:S(2)}) async-start(bf16[16,1,48,256]{3,2,1,0:T(8,128)(2,1)} %bitcast.34), calls=%async_computation.5 | async-start | bytes 786432 | tf_op jit(solution)/shard_map/all_to_all | solution.py:80
  374.0 20.1 %all-to-all-done.4 = bf16[16,1,48,256]{3,2,1,0:T(8,128)(2,1)S(1)} async-done(((bf16[16,1,48,256]{3,2,1,0:T(8,128)(2,1)}), bf16[16,1,48,256]{3,2,1,0:T(8,128)(2,1)S(1)}, u32[]{:S(2)}, u32[]{:S(2)}) %all-to-all-start.4) | async-done | bytes 393248 | tf_op jit(solution)/shard_map/all_to_all | solution.py:80
  394.1 1.9 gather_fusion.4
  397.8 16.1 %psum.15 = f32[256]{0:T(256)S(1)} all-reduce(f32[256]{0:T(256)S(1)} %multiply_reduce_fusion.1), channel_id=1, replica_groups=mesh['ep'=16,'mx'=4,'my'=8] {'my'}, use_global_device_ids=true, to_apply=%region_10.11 | all-reduce | flops 256 | bytes 2048 | tf_op jit(solution)/shard_map/psum | solution.py:16
  (63 shorter events, 8.9 us)
Async XLA Ops:
  7.2 6.2 %copy-start = (bf16[256,2048]{1,0:T(8,128)(2,1)S(1)}, bf16[256,2048]{1,0:T(8,128)(2,1)}, u32[]{:S(2)}) copy-start(bf16[256,2048]{1,0:T(8,128)(2,1)} %param.14) | copy-start | bytes 3145732
  7.2 23.0 %copy-start.6 = (f32[256]{0:T(256)S(1)}, f32[256]{0:T(256)}, u32[]{:S(2)}) copy-start(f32[256]{0:T(256)} %param.17) | copy-start | bytes 3076
  15.1 33.7 %copy-start.8 = (s32[16]{0:T(128)S(1)}, s32[16]{0:T(128)}, u32[]{:S(2)}) copy-start(s32[16]{0:T(128)} %constant.78) | copy-start | bytes 196
  15.1 33.7 %copy-start.1 = (bf16[8,44,512]{2,0,1:T(8,128)(2,1)S(1)}, bf16[8,44,512]{2,0,1:T(8,128)(2,1)}, u32[]{:S(2)}) copy-start(bf16[8,44,512]{2,0,1:T(8,128)(2,1)} %param.18) | copy-start | bytes 1081348
  33.6 36.2 %all-to-all-start = ((bf16[16,1,48,256]{3,2,1,0:T(8,128)(2,1)}), bf16[16,1,48,256]{3,2,1,0:T(8,128)(2,1)S(1)}, u32[]{:S(2)}, u32[]{:S(2)}) async-start(bf16[16,1,48,256]{3,2,1,0:T(8,128)(2,1)} %bitcast.5), calls=%async_computation | async-start | bytes 786432 | tf_op jit(solution)/shard_map/all_to_all | solution.py:55
  48.8 168.3 %all-gather.7.cloned.1.call-start = ((), (), s32[]{:S(2)}) async-start(), calls=%async_computation.7 | async-start | bytes 3932160 | tf_op jit(solution)/shard_map/all_gather | solution.py:64
  51.5 66.1 %copy-start.2 = (bf16[8,44,512]{2,0,1:T(8,128)(2,1)S(1)}, bf16[8,44,512]{2,0,1:T(8,128)(2,1)}, u32[]{:S(2)}) copy-start(bf16[8,44,512]{2,0,1:T(8,128)(2,1)} %param.19) | copy-start | bytes 1081348
  69.8 47.0 %copy-start.4 = (bf16[16,1,48,256]{3,2,1,0:T(8,128)(2,1)}, bf16[16,1,48,256]{3,2,1,0:T(8,128)(2,1)S(1)}, u32[]{:S(2)}) copy-start(bf16[16,1,48,256]{3,2,1,0:T(8,128)(2,1)S(1)} %all-to-all-done) | copy-start | bytes 1179652
  116.7 104.7 %all-gather.5.cloned.1.call-start = ((), (), s32[]{:S(2)}) async-start(), calls=%async_computation.6 | async-start | bytes 3538944 | tf_op jit(solution)/shard_map/all_gather | solution.py:56
  117.5 133.1 %all-gather.9.cloned.1.call-start = ((), (), s32[]{:S(2)}) async-start(), calls=%async_computation.8 | async-start | bytes 3932160 | tf_op jit(solution)/shard_map/all_gather | solution.py:64
  120.2 47.2 %copy-start.3 = (bf16[8,44,512]{2,0,1:T(8,128)(2,1)S(1)}, bf16[8,44,512]{2,0,1:T(8,128)(2,1)}, u32[]{:S(2)}) copy-start(bf16[8,44,512]{2,0,1:T(8,128)(2,1)} %param.20) | copy-start | bytes 1081348
  167.1 132.9 %all-gather.11.cloned.1.call-start = ((), (), s32[]{:S(2)}) async-start(), calls=%async_computation.9 | async-start | bytes 3932160 | tf_op jit(solution)/shard_map/all_gather | solution.py:64
  217.0 144.5 %reduce-scatter.2.cloned.1.call-start = ((), (), s32[]{:S(2)}) async-start(), calls=%async_computation.10 | async-start | bytes 3538944 | tf_op jit(solution)/shard_map/reduce_scatter | solution.py:75
  316.9 56.9 %copy-start.5 = (f32[256,2]{0,1:T(2,128)S(1)}, f32[256,2]{0,1:T(2,128)}, u32[]{:S(2)}) copy-start(f32[256,2]{0,1:T(2,128)} %param.22) | copy-start | bytes 6148
  361.5 32.6 %all-to-all-start.4 = ((bf16[16,1,48,256]{3,2,1,0:T(8,128)(2,1)}), bf16[16,1,48,256]{3,2,1,0:T(8,128)(2,1)S(1)}, u32[]{:S(2)}, u32[]{:S(2)}) async-start(bf16[16,1,48,256]{3,2,1,0:T(8,128)(2,1)} %bitcast.34), calls=%async_computation.5 | async-start | bytes 786432 | tf_op jit(solution)/shard_map/all_to_all | solution.py:80
  373.8 40.1 %copy-start.7 = (f32[256]{0:T(256)S(1)}, f32[256]{0:T(256)}, u32[]{:S(2)}) copy-start(f32[256]{0:T(256)} %param.23) | copy-start | bytes 3076
Sparse Core Ops, SparseCore 0:
  116.9 41.5 all-gather.6
  160.6 40.3 all-gather.4
  203.1 47.4 all-gather.8
  252.5 47.4 all-gather.10
  317.0 44.4 reduce-scatter.1
where the time goes:
time: 422 us; the launch traced here: 421 us
  blocking collectives  171 us (41%)
  waiting for transfers between devices  151 us (36%)
  local copies, waits for them, and re-layouts  31.9 us (8%)
  starting transfers between devices  27.9 us (7%)
  matrix products  21.1 us (5%)
  between operations  14.1 us (3%)
  other arithmetic  4.43 us (1%)
    all_to_all x3, blocking collectives, fetch(): lax.all_to_all(chosen_rows, 'ep', split_axis=0, concat_axis=0, tiled=True)  140 us
    all_gather x3, waiting for transfers between devices, fetch(): wide = lax.all_gather(got, 'mx', axis=3, tiled=True)  67.4 us
    reduce_scatter x1, waiting for transfers between devices, shards(): lax.psum_scatter(expert_out.astype(jnp.bfloat16), 'my', scatter_dimension...  44.6 us
    psum x2, blocking collectives, row_scale(): row_total = lax.psum(partial_sq, 'my')  31.1 us
    all_to_all x1, waiting for transfers between devices, shards(): lax.all_to_all(sent_back, 'ep', split_axis=0, concat_axis=0, tiled=True)  20.1 us
    all_to_all x1, waiting for transfers between devices, shards(): lax.all_to_all(packed, 'ep', split_axis=0, concat_axis=0, tiled=True)  18.3 us
    all_to_all x1, starting transfers between devices, shards(): lax.all_to_all(packed, 'ep', split_axis=0, concat_axis=0, tiled=True)  15.2 us
    another operation x4, local copies, waits for them, and re-layouts  13.1 us
  transfers between devices with their start and end apart: 7, of which 5 were waited for; matrix products, arithmetic and copies ran while one was open for 6% of the time, Pallas kernels for 0%

commit v1 on v0

--- a/solution.py
+++ b/solution.py
@@ -61,7 +61,9 @@
     def fetch(weight, after):
         chosen_rows, _ = lax.optimization_barrier((weight[expert_table], after))
         got = lax.all_to_all(chosen_rows, "ep", split_axis=0, concat_axis=0, tiled=True)
-        wide = lax.all_gather(got, "mx", axis=3, tiled=True)
+        wide = jnp.concatenate(
+            lax.all_to_all(jnp.stack([got] * lax.axis_size("mx")), "mx", 0, 0), axis=3
+        )
         return (got, jnp.transpose(wide, (1, 0, 2, 3)).reshape(slot_dev, ep_count * piece_units, D))
 
     raw_gate, w_gate = fetch(gate_weight, landed)

time: 422 us -> 455 us (1.078)
  the two profiles are of different devices: /device:TPU:2 before, /device:TPU:6 now
where the time goes in v1:
time: 455 us; the launch traced here: 453 us
  waiting for transfers between devices  261 us (57%)
  starting transfers between devices  73 us (16%)
  local copies, waits for them, and re-layouts  50.1 us (11%)
  blocking collectives  31.8 us (7%)
  matrix products  19 us (4%)
  between operations  14.4 us (3%)
    all_to_all x3, waiting for transfers between devices, fetch(): lax.all_to_all(chosen_rows, 'ep', split_axis=0, concat_axis=0, tiled=True)  110 us
    all_to_all x3, waiting for transfers between devices, fetch(): lax.all_to_all(jnp.stack([got] * lax.axis_size('mx')), 'mx', 0, 0)  60.2 us
    reduce_scatter x1, waiting for transfers between devices, shards(): lax.psum_scatter(expert_out.astype(jnp.bfloat16), 'my', scatter_dimension...  51.5 us
    psum x2, blocking collectives, row_scale(): row_total = lax.psum(partial_sq, 'my')  31.8 us
    all_to_all x3, starting transfers between devices, fetch(): lax.all_to_all(chosen_rows, 'ep', split_axis=0, concat_axis=0, tiled=True)  27.1 us
    all_to_all x1, waiting for transfers between devices, shards(): lax.all_to_all(sent_back, 'ep', split_axis=0, concat_axis=0, tiled=True)  20 us
    all_to_all x3, starting transfers between devices, fetch(): lax.all_to_all(jnp.stack([got] * lax.axis_size('mx')), 'mx', 0, 0)  18.4 us
    all_to_all x1, waiting for transfers between devices, shards(): lax.all_to_all(packed, 'ep', split_axis=0, concat_axis=0, tiled=True)  18.3 us
  transfers between devices with their start and end apart: 10, of which 9 were waited for; matrix products, arithmetic and copies ran while one was open for 7% of the time, Pallas kernels for 0%

profile of v1, /device:TPU:6, one launch (start us, length us, event | category | flops | bytes accessed | tf_op | source)
XLA Modules:
  0.0 453.5 jit_solution(18324850280351187720)
XLA Ops:
  15.2 15.0 %psum.14 = f32[256]{0:T(256)S(1)} all-reduce(f32[256]{0:T(256)S(1)} %get-tuple-element.10), channel_id=1, replica_groups=mesh['ep'=16,'mx'=4,'my'=8] {'my'}, use_global_device_ids=true, to_apply=%region_2.0 | all-reduce | flops 256 | bytes 2048 | tf_op jit(solution)/shard_map/psum | solution.py:16
  33.6 15.2 %all-to-all-start = ((bf16[16,1,48,256]{3,2,1,0:T(8,128)(2,1)}), bf16[16,1,48,256]{3,2,1,0:T(8,128)(2,1)S(1)}, u32[]{:S(2)}, u32[]{:S(2)}) async-start(bf16[16,1,48,256]{3,2,1,0:T(8,128)(2,1)} %bitcast.5), calls=%async_computation | async-start | bytes 786432 | tf_op jit(solution)/shard_map/all_to_all | solution.py:55
  51.5 18.3 %all-to-all-done = bf16[16,1,48,256]{3,2,1,0:T(8,128)(2,1)S(1)} async-done(((bf16[16,1,48,256]{3,2,1,0:T(8,128)(2,1)}), bf16[16,1,48,256]{3,2,1,0:T(8,128)(2,1)S(1)}, u32[]{:S(2)}, u32[]{:S(2)}) %all-to-all-start) | async-done | bytes 393248 | tf_op jit(solution)/shard_map/all_to_all | solution.py:55
  71.1 6.5 %all-to-all-start.1 = ((bf16[16,1,44,512]{3,2,1,0:T(8,128)(2,1)}), bf16[16,1,44,512]{3,2,1,0:T(8,128)(2,1)S(1)}, u32[]{:S(2)}, u32[]{:S(2)}) async-start(bf16[16,1,44,512]{3,2,1,0:T(8,128)(2,1)} %copy.44), calls=%async_computation.1 | async-start | bytes 1572864 | tf_op jit(solution)/shard_map/all_to_all | solution.py:63
  80.3 34.9 %all-to-all-done.1 = bf16[16,1,44,512]{3,2,1,0:T(8,128)(2,1)S(1)} async-done(((bf16[16,1,44,512]{3,2,1,0:T(8,128)(2,1)}), bf16[16,1,44,512]{3,2,1,0:T(8,128)(2,1)S(1)}, u32[]{:S(2)}, u32[]{:S(2)}) %all-to-all-start.1) | async-done | bytes 720928 | tf_op jit(solution)/shard_map/all_to_all | solution.py:63
  116.5 8.1 %all-to-all-start.3 = ((bf16[16,1,44,512]{3,2,1,0:T(8,128)(2,1)}), bf16[16,1,44,512]{3,2,1,0:T(8,128)(2,1)S(1)}, u32[]{:S(2)}, u32[]{:S(2)}) async-start(bf16[16,1,44,512]{3,2,1,0:T(8,128)(2,1)} %copy.47), calls=%async_computation.3 | async-start | bytes 1572864 | tf_op jit(solution)/shard_map/all_to_all | solution.py:63
  125.8 38.1 %all-to-all-done.3 = bf16[16,1,44,512]{3,2,1,0:T(8,128)(2,1)S(1)} async-done(((bf16[16,1,44,512]{3,2,1,0:T(8,128)(2,1)}), bf16[16,1,44,512]{3,2,1,0:T(8,128)(2,1)S(1)}, u32[]{:S(2)}, u32[]{:S(2)}) %all-to-all-start.3) | async-done | bytes 720928 | tf_op jit(solution)/shard_map/all_to_all | solution.py:63
  166.9 5.2 %all-to-all-start.2 = ((bf16[4,16,1,44,512]{4,1,3,2,0:T(8,128)(2,1)}), bf16[4,16,1,44,512]{4,1,3,2,0:T(8,128)(2,1)}, u32[]{:S(2)}, u32[]{:S(2)}) async-start(bf16[4,16,1,44,512]{4,1,3,2,0:T(8,128)(2,1)} %stack.6), calls=%async_computation.2 | async-start | bytes 5767168 | tf_op jit(solution)/shard_map/all_to_all | solution.py:65
  176.0 24.0 %all-to-all-done.2 = bf16[4,16,1,44,512]{4,1,3,2,0:T(8,128)(2,1)} async-done(((bf16[4,16,1,44,512]{4,1,3,2,0:T(8,128)(2,1)}), bf16[4,16,1,44,512]{4,1,3,2,0:T(8,128)(2,1)}, u32[]{:S(2)}, u32[]{:S(2)}) %all-to-all-start.2) | async-done | bytes 2883616 | tf_op jit(solution)/shard_map/all_to_all | solution.py:65
  200.0 12.5 %all-to-all-start.5 = ((bf16[16,1,44,512]{3,2,1,0:T(8,128)(2,1)}), bf16[16,1,44,512]{3,2,1,0:T(8,128)(2,1)S(1)}, u32[]{:S(2)}, u32[]{:S(2)}) async-start(bf16[16,1,44,512]{3,2,1,0:T(8,128)(2,1)} %copy.50), calls=%async_computation.5 | async-start | bytes 1572864 | tf_op jit(solution)/shard_map/all_to_all | solution.py:63
  213.6 37.1 %all-to-all-done.5 = bf16[16,1,44,512]{3,2,1,0:T(8,128)(2,1)S(1)} async-done(((bf16[16,1,44,512]{3,2,1,0:T(8,128)(2,1)}), bf16[16,1,44,512]{3,2,1,0:T(8,128)(2,1)S(1)}, u32[]{:S(2)}, u32[]{:S(2)}) %all-to-all-start.5) | async-done | bytes 720928 | tf_op jit(solution)/shard_map/all_to_all | solution.py:63
  252.6 6.6 %all-to-all-start.4 = ((bf16[4,16,1,44,512]{4,1,3,2,0:T(8,128)(2,1)}), bf16[4,16,1,44,512]{4,1,3,2,0:T(8,128)(2,1)}, u32[]{:S(2)}, u32[]{:S(2)}) async-start(bf16[4,16,1,44,512]{4,1,3,2,0:T(8,128)(2,1)} %stack.7), calls=%async_computation.4 | async-start | bytes 5767168 | tf_op jit(solution)/shard_map/all_to_all | solution.py:65
  259.7 27.5 %all-to-all-done.4 = bf16[4,16,1,44,512]{4,1,3,2,0:T(8,128)(2,1)} async-done(((bf16[4,16,1,44,512]{4,1,3,2,0:T(8,128)(2,1)}), bf16[4,16,1,44,512]{4,1,3,2,0:T(8,128)(2,1)}, u32[]{:S(2)}, u32[]{:S(2)}) %all-to-all-start.4) | async-done | bytes 2883616 | tf_op jit(solution)/shard_map/all_to_all | solution.py:65
  289.1 6.6 %all-to-all-start.6 = ((bf16[4,16,1,44,512]{4,1,3,2,0:T(8,128)(2,1)}), bf16[4,16,1,44,512]{4,1,3,2,0:T(8,128)(2,1)}, u32[]{:S(2)}, u32[]{:S(2)}) async-start(bf16[4,16,1,44,512]{4,1,3,2,0:T(8,128)(2,1)} %stack.8), calls=%async_computation.6 | async-start | bytes 5767168 | tf_op jit(solution)/shard_map/all_to_all | solution.py:65
  295.7 4.0 copy.46
  302.3 5.2 %fusion.14 = f32[768,704]{0,1:T(8,128)S(1)} fusion(bf16[768,2048]{1,0:T(8,128)(2,1)} %bitcast.65, bf16[704,2048]{1,0:T(8,128)(2,1)} %bitcast.59), kind=kOutput, calls=%fused_computation.50 | convolution fusion | flops 2214592512 | bytes 8192000 | tf_op jit(solution)/shard_map/srd,sfd->srf/dot_general | solution.py:73
  307.5 4.0 copy.49
  314.0 8.7 %all-to-all-done.6 = bf16[4,16,1,44,512]{4,1,3,2,0:T(8,128)(2,1)} async-done(((bf16[4,16,1,44,512]{4,1,3,2,0:T(8,128)(2,1)}), bf16[4,16,1,44,512]{4,1,3,2,0:T(8,128)(2,1)}, u32[]{:S(2)}, u32[]{:S(2)}) %all-to-all-start.6) | async-done | bytes 2883616 | tf_op jit(solution)/shard_map/all_to_all | solution.py:65
  322.7 4.0 copy.52
  329.2 12.0 %fusion = bf16[1,768,2048]{2,1,0:T(8,128)(2,1)} fusion(bf16[704,2048]{1,0:T(8,128)(2,1)} %bitcast.60, f32[768,704]{0,1:T(8,128)S(1)} %fusion.14, bf16[768,2048]{1,0:T(8,128)(2,1)} %bitcast.66, bf16[704,2048]{1,0:T(8,128)(2,1)} %bitcast.58), kind=kOutput, calls=%fused_computation.7 | convolution fusion | flops 4434001920 | bytes 14221312 | tf_op jit(solution)/shard_map/srf,sfd->srd/dot_general | solution.py:76
  341.3 51.5 %reduce-scatter.2.cloned.1.call-done = bf16[1,768,256]{2,1,0:T(8,128)(2,1)} async-done(((bf16[1,768,2048]{2,1,0:T(8,128)(2,1)}), bf16[1,768,256]{2,1,0:T(8,128)(2,1)}) %reduce-scatter.2.cloned.1.call-update) | async-done | bytes 393232 | tf_op jit(solution)/shard_map/reduce_scatter | solution.py:77
  392.8 12.3 %all-to-all-start.7 = ((bf16[16,1,48,256]{3,2,1,0:T(8,128)(2,1)}), bf16[16,1,48,256]{3,2,1,0:T(8,128)(2,1)S(1)}, u32[]{:S(2)}, u32[]{:S(2)}) async-start(bf16[16,1,48,256]{3,2,1,0:T(8,128)(2,1)} %bitcast.61), calls=%async_computation.8 | async-start | bytes 786432 | tf_op jit(solution)/shard_map/all_to_all | solution.py:82
  405.3 20.0 %all-to-all-done.7 = bf16[16,1,48,256]{3,2,1,0:T(8,128)(2,1)S(1)} async-done(((bf16[16,1,48,256]{3,2,1,0:T(8,128)(2,1)}), bf16[16,1,48,256]{3,2,1,0:T(8,128)(2,1)S(1)}, u32[]{:S(2)}, u32[]{:S(2)}) %all-to-all-start.7) | async-done | bytes 393248 | tf_op jit(solution)/shard_map/all_to_all | solution.py:82
  429.1 16.8 %psum.15 = f32[256]{0:T(256)S(1)} all-reduce(f32[256]{0:T(256)S(1)} %multiply_reduce_fusion.1), channel_id=1, replica_groups=mesh['ep'=16,'mx'=4,'my'=8] {'my'}, use_global_device_ids=true, to_apply=%region_10.11 | all-reduce | flops 256 | bytes 2048 | tf_op jit(solution)/shard_map/psum | solution.py:16
  (76 shorter events, 44.9 us)
Async XLA Ops:
  7.2 6.2 %copy-start = (bf16[256,2048]{1,0:T(8,128)(2,1)S(1)}, bf16[256,2048]{1,0:T(8,128)(2,1)}, u32[]{:S(2)}) copy-start(bf16[256,2048]{1,0:T(8,128)(2,1)} %param.14) | copy-start | bytes 3145732
  7.2 23.0 %copy-start.8 = (f32[256]{0:T(256)S(1)}, f32[256]{0:T(256)}, u32[]{:S(2)}) copy-start(f32[256]{0:T(256)} %param.17) | copy-start | bytes 3076
  15.1 15.0 %copy-start.4 = (f32[256,256]{1,0:T(8,128)}, f32[256,256]{1,0:T(8,128)S(1)}, u32[]{:S(2)}) copy-start(f32[256,256]{1,0:T(8,128)S(1)} %get-tuple-element.11) | copy-start | bytes 786436
  15.1 33.6 %copy-start.10 = (s32[16]{0:T(128)S(1)}, s32[16]{0:T(128)}, u32[]{:S(2)}) copy-start(s32[16]{0:T(128)} %constant.78) | copy-start | bytes 196
  15.2 33.7 %copy-start.1 = (bf16[8,44,512]{2,0,1:T(8,128)(2,1)S(1)}, bf16[8,44,512]{2,0,1:T(8,128)(2,1)}, u32[]{:S(2)}) copy-start(bf16[8,44,512]{2,0,1:T(8,128)(2,1)} %param.18) | copy-start | bytes 1081348
  33.6 36.2 %all-to-all-start = ((bf16[16,1,48,256]{3,2,1,0:T(8,128)(2,1)}), bf16[16,1,48,256]{3,2,1,0:T(8,128)(2,1)S(1)}, u32[]{:S(2)}, u32[]{:S(2)}) async-start(bf16[16,1,48,256]{3,2,1,0:T(8,128)(2,1)} %bitcast.5), calls=%async_computation | async-start | bytes 786432 | tf_op jit(solution)/shard_map/all_to_all | solution.py:55
  51.4 26.2 %copy-start.2 = (bf16[8,44,512]{2,0,1:T(8,128)(2,1)S(1)}, bf16[8,44,512]{2,0,1:T(8,128)(2,1)}, u32[]{:S(2)}) copy-start(bf16[8,44,512]{2,0,1:T(8,128)(2,1)} %param.19) | copy-start | bytes 1081348
  69.8 10.5 %copy-start.6 = (bf16[16,1,48,256]{3,2,1,0:T(8,128)(2,1)}, bf16[16,1,48,256]{3,2,1,0:T(8,128)(2,1)S(1)}, u32[]{:S(2)}) copy-start(bf16[16,1,48,256]{3,2,1,0:T(8,128)(2,1)S(1)} %all-to-all-done) | copy-start | bytes 1179652
  71.1 44.1 %all-to-all-start.1 = ((bf16[16,1,44,512]{3,2,1,0:T(8,128)(2,1)}), bf16[16,1,44,512]{3,2,1,0:T(8,128)(2,1)S(1)}, u32[]{:S(2)}, u32[]{:S(2)}) async-start(bf16[16,1,44,512]{3,2,1,0:T(8,128)(2,1)} %copy.44), calls=%async_computation.1 | async-start | bytes 1572864 | tf_op jit(solution)/shard_map/all_to_all | solution.py:63
  116.5 47.4 %all-to-all-start.3 = ((bf16[16,1,44,512]{3,2,1,0:T(8,128)(2,1)}), bf16[16,1,44,512]{3,2,1,0:T(8,128)(2,1)S(1)}, u32[]{:S(2)}, u32[]{:S(2)}) async-start(bf16[16,1,44,512]{3,2,1,0:T(8,128)(2,1)} %copy.47), calls=%async_computation.3 | async-start | bytes 1572864 | tf_op jit(solution)/shard_map/all_to_all | solution.py:63
  166.9 5.2 %copy-start.3 = (bf16[8,44,512]{2,0,1:T(8,128)(2,1)S(1)}, bf16[8,44,512]{2,0,1:T(8,128)(2,1)}, u32[]{:S(2)}) copy-start(bf16[8,44,512]{2,0,1:T(8,128)(2,1)} %param.20) | copy-start | bytes 1081348
  166.9 33.1 %all-to-all-start.2 = ((bf16[4,16,1,44,512]{4,1,3,2,0:T(8,128)(2,1)}), bf16[4,16,1,44,512]{4,1,3,2,0:T(8,128)(2,1)}, u32[]{:S(2)}, u32[]{:S(2)}) async-start(bf16[4,16,1,44,512]{4,1,3,2,0:T(8,128)(2,1)} %stack.6), calls=%async_computation.2 | async-start | bytes 5767168 | tf_op jit(solution)/shard_map/all_to_all | solution.py:65
  200.0 50.7 %all-to-all-start.5 = ((bf16[16,1,44,512]{3,2,1,0:T(8,128)(2,1)}), bf16[16,1,44,512]{3,2,1,0:T(8,128)(2,1)S(1)}, u32[]{:S(2)}, u32[]{:S(2)}) async-start(bf16[16,1,44,512]{3,2,1,0:T(8,128)(2,1)} %copy.50), calls=%async_computation.5 | async-start | bytes 1572864 | tf_op jit(solution)/shard_map/all_to_all | solution.py:63
  212.5 89.8 %all-gather.2.cloned.1.call-start = ((), (), s32[]{:S(2)}) async-start(), calls=%async_computation.9 | async-start | bytes 3538944 | tf_op jit(solution)/shard_map/all_gather | solution.py:56
  252.6 34.5 %all-to-all-start.4 = ((bf16[4,16,1,44,512]{4,1,3,2,0:T(8,128)(2,1)}), bf16[4,16,1,44,512]{4,1,3,2,0:T(8,128)(2,1)}, u32[]{:S(2)}, u32[]{:S(2)}) async-start(bf16[4,16,1,44,512]{4,1,3,2,0:T(8,128)(2,1)} %stack.7), calls=%async_computation.4 | async-start | bytes 5767168 | tf_op jit(solution)/shard_map/all_to_all | solution.py:65
  289.1 33.6 %all-to-all-start.6 = ((bf16[4,16,1,44,512]{4,1,3,2,0:T(8,128)(2,1)}), bf16[4,16,1,44,512]{4,1,3,2,0:T(8,128)(2,1)}, u32[]{:S(2)}, u32[]{:S(2)}) async-start(bf16[4,16,1,44,512]{4,1,3,2,0:T(8,128)(2,1)} %stack.8), calls=%async_computation.6 | async-start | bytes 5767168 | tf_op jit(solution)/shard_map/all_to_all | solution.py:65
  295.7 97.0 %reduce-scatter.2.cloned.1.call-start = ((), (), s32[]{:S(2)}) async-start(), calls=%async_computation.10 | async-start | bytes 3538944 | tf_op jit(solution)/shard_map/reduce_scatter | solution.py:77
  341.3 63.8 %copy-start.7 = (f32[256,2]{0,1:T(2,128)S(1)}, f32[256,2]{0,1:T(2,128)}, u32[]{:S(2)}) copy-start(f32[256,2]{0,1:T(2,128)} %param.22) | copy-start | bytes 6148
  341.3 87.0 %copy-start.5 = (f32[256,256]{1,0:T(8,128)S(1)}, f32[256,256]{1,0:T(8,128)}, u32[]{:S(2)}) copy-start(f32[256,256]{1,0:T(8,128)} %copy-done.4) | copy-start | bytes 786436
  392.8 32.5 %all-to-all-start.7 = ((bf16[16,1,48,256]{3,2,1,0:T(8,128)(2,1)}), bf16[16,1,48,256]{3,2,1,0:T(8,128)(2,1)S(1)}, u32[]{:S(2)}, u32[]{:S(2)}) async-start(bf16[16,1,48,256]{3,2,1,0:T(8,128)(2,1)} %bitcast.61), calls=%async_computation.8 | async-start | bytes 786432 | tf_op jit(solution)/shard_map/all_to_all | solution.py:82
  405.1 40.8 %copy-start.9 = (f32[256]{0:T(256)S(1)}, f32[256]{0:T(256)}, u32[]{:S(2)}) copy-start(f32[256]{0:T(256)} %param.23) | copy-start | bytes 3076
Sparse Core Ops, SparseCore 0:
  215.4 40.9 all-gather.1
  341.4 51.3 reduce-scatter.1
